TPU v7x, 256 devices: a whole 4x4x8 slice. The times are simulated.
256 devices in a mesh: chan: 128 (over x_lo, z, y, core), tm: 2 (over x_hi).
Axes of the slice: x: 4 (x_hi: 2, x_lo: 2; x = x_hi * 2 + x_lo), y: 4, z: 8, core: 2. Of those that a mesh axis runs over, the one named last changes fastest.
Arguments:
- records: bfloat16 [6, 2048, 16384], P('tm', None, 'chan'), may hold values from -600 to 600
- band_taps: float32 [64], replicated, may hold values from -0.75 to 0.75
- white_taps: float32 [16, 16384], P(None, 'chan'), may hold values from -1.5 to 1.5
- live_mask: int32 [16384], P('chan'), may hold values 0 or 1
- partners: int32 [6, 128], P(None, 'chan'), may hold values from 0 to 127, as said below
Outputs:
- correlations: float32 [6, 32, 16384, 128], P(None, 'tm', 'chan')
Inputs may be any that keep to these rules, and one draw needn't show every extreme that they name: In each round blocks are matched in pairs: partners[r, b] differs from b, partners[r, partners[r, b]] = b, and partners[r, b] - b equals d or -d modulo 128, with the same d in the finite set (1, 2, 4) for all blocks of the round. Over all rounds every block b is matched with b + 1, b - 1, b + 2, b - 2, b + 4 and b - 4 modulo 128, each once.
All inputs are finite; a program needn't handle non-finite values. No bound on the sum of `live_mask` on one device may be relied on, other than what follows from the above.
Results may differ from a plain program's by a relative error of at most 0.0058.
Values may be sent and summed in bfloat16 or wider, within the bound.
No kernel may reach another device: no remote copies, remote signals or barrier semaphores. Data moves between devices by JAX's collectives and lax.ppermute only.
A program may use at most 64 MiB of HBM per device.

v0:
```python
import math
import jax
import jax.numpy as jnp
from jax import lax
from jax.sharding import PartitionSpec as P

NB = 128
SEG = 6
LAGS = 32


def shifted(value, axis, steps):
    count = lax.axis_size(axis)
    pairs = [(source, (source + steps) % count) for source in range(count)]
    return lax.ppermute(value, axis, pairs)


def bin_numbers(samples, bin_count):
    return samples // 64 + samples // (4 * bin_count) * jnp.arange(bin_count, dtype=jnp.int32)


def rotation(products, samples):
    angles = jnp.mod(products, samples).astype(jnp.float32) * (2.0 * math.pi / samples)
    return (jnp.cos(angles), jnp.sin(angles))


def dft_table(samples, bin_index):
    sample_index = jnp.arange(samples, dtype=jnp.int32)
    cos_part, sin_part = rotation(sample_index[:, None] * bin_index[None, :], samples)
    return jnp.concatenate([cos_part, -sin_part], axis=1).astype(jnp.bfloat16)


def responses(band_taps, white_taps, bin_index, samples):
    highest = lax.Precision.HIGHEST
    band_cos, band_sin = rotation(
        jnp.arange(band_taps.shape[0], dtype=jnp.int32)[:, None] * bin_index[None, :], samples
    )
    white_cos, white_sin = rotation(
        jnp.arange(white_taps.shape[0], dtype=jnp.int32)[:, None] * bin_index[None, :], samples
    )
    band_real = jnp.dot(band_taps, band_cos, precision=highest)
    band_imag = -jnp.dot(band_taps, band_sin, precision=highest)
    white_real = jnp.dot(white_taps.T, white_cos, precision=highest)
    white_imag = -jnp.dot(white_taps.T, white_sin, precision=highest)
    resp_real = white_real * band_real[None, :] - white_imag * band_imag[None, :]
    resp_imag = white_real * band_imag[None, :] + white_imag * band_real[None, :]
    return (resp_real, resp_imag)


def filtered(raw_spec, resp_real, resp_imag, live_values):
    bin_count = resp_real.shape[1]
    spec_real = raw_spec[..., :bin_count]
    spec_imag = raw_spec[..., bin_count:]
    real_resp = resp_real[:, None, :]
    imag_resp = resp_imag[:, None, :]
    out_real = (real_resp * spec_real - imag_resp * spec_imag) * live_values[:, None, None]
    out_imag = (real_resp * spec_imag + imag_resp * spec_real) * live_values[:, None, None]
    return jnp.concatenate([out_real, out_imag], axis=2).astype(jnp.bfloat16)


def inverse_norms(flat_rows):
    values = flat_rows.astype(jnp.float32)
    mean_square = jnp.sum(values * values, axis=-1) / (SEG * NB)
    return lax.rsqrt(mean_square + 1e-06)


def turned_rows(own_block, lag_values, bin_index, samples):
    lag_cos, lag_sin = rotation(lag_values[:, None] * bin_index[None, :], samples)
    values = own_block.astype(jnp.float32).reshape(own_block.shape[0], SEG, 2, NB)
    part_real = values[:, :, 0, :][None]
    part_imag = values[:, :, 1, :][None]
    cos_factor = lag_cos[:, None, None, :]
    sin_factor = lag_sin[:, None, None, :]
    new_real = part_real * cos_factor - part_imag * sin_factor
    new_imag = part_real * sin_factor + part_imag * cos_factor
    stacked = jnp.stack([new_real, new_imag], axis=3)
    return stacked.astype(jnp.bfloat16).reshape(lag_values.shape[0] * own_block.shape[0], -1)


def tile_sums(turned, chosen, own_scale, part_scale, lag_count):
    rounds, row_count, inner_size = chosen.shape
    flat_rows = chosen.reshape(rounds * row_count, inner_size)
    tile_totals = lax.dot_general(
        turned, flat_rows, (((1,), (1,)), ((), ())), preferred_element_type=jnp.float32
    )
    tile_totals = tile_totals.reshape(lag_count, row_count, rounds, row_count)
    scaled = (
        tile_totals
        * own_scale[None, :, None, None]
        * part_scale[None, None, :, :]
        * (1.0 / math.sqrt(SEG * NB))
    )
    return jnp.transpose(scaled, (2, 0, 1, 3))


def local(records, band_taps, white_taps, live_mask, partners):
    samples = records.shape[1]
    channels = records.shape[2]
    bin_index = bin_numbers(samples, NB)
    transform = dft_table(samples, bin_index)
    resp_real, resp_imag = responses(band_taps, white_taps, bin_index, samples)
    live_values = live_mask.astype(jnp.float32)
    raw_spec = jnp.einsum(
        "stc,tf->csf",
        lax.all_gather(records, "tm", axis=0, tiled=True),
        transform,
        preferred_element_type=jnp.float32,
    )
    spectra = filtered(raw_spec, resp_real, resp_imag, live_values)
    own_block = spectra.reshape(channels, -1)
    my_block = lax.axis_index("chan")
    block_count = lax.axis_size("chan")
    offset_list = (-4, -2, -1, 1, 2, 4)
    pieces = {}
    for offset in (1, 2, 4, -1, -2, -4):
        pieces[offset] = shifted(own_block, "chan", -offset)
    window = jnp.stack([pieces[offset] for offset in offset_list])
    delta = jnp.mod(partners[:, 0] - my_block + block_count // 2, block_count) - block_count // 2
    slot_index = jnp.zeros_like(delta)
    for position, offset in enumerate(offset_list):
        slot_index = slot_index + position * (delta == offset).astype(jnp.int32)
    chosen = jnp.take(window, slot_index, axis=0)
    own_scale = inverse_norms(own_block)
    part_scale = inverse_norms(chosen)
    lag_count = LAGS // lax.axis_size("tm")
    lag_first = lax.axis_index("tm") * lag_count
    lag_values = 3 * (lag_first + jnp.arange(lag_count, dtype=jnp.int32) - LAGS // 2)
    turned = turned_rows(own_block, lag_values, bin_index, samples)
    return tile_sums(turned, chosen, own_scale, part_scale, lag_count)


def solution(mesh):
    return jax.shard_map(
        local,
        mesh=mesh,
        in_specs=(P("tm", None, "chan"), P(), P(None, "chan"), P("chan"), P(None, "chan")),
        out_specs=P(None, "tm", "chan", None),
        check_vma=False,
    )
```

profile of v0, /device:TPU:2, one launch (start us, length us, event | category | flops | bytes accessed | tf_op | source)
XLA Modules:
  0.0 153.6 jit_solution(10691760521809553635)
XLA Ops:
  6.5 0.7 all-gather.2.cloned.1.call-update
  7.9 0.7 and_bitcast_fusion
  8.6 0.9 convolution_bitcast_fusion.2
  9.6 0.9 fusion.5
  11.4 4.9 %cosine_convert_fusion = (bf16[2048,128]{0,1:T(8,128)(2,1)S(1)}, bf16[2048,128]{0,1:T(8,128)(2,1)S(1)}) fusion(s32[128]{0:T(128)S(1)} %multiply_add_fusion), kind=kLoop, calls=%fused_computation.25 | loop fusion | flops 4456448 | bytes 1049088 | tf_op jit(solution)/shard_map/convert.3
  16.2 46.5 %all-gather.2.cloned.1.call-done = bf16[6,2048,128]{2,1,0:T(8,128)(2,1)} async-done(((bf16[3,2048,128]{2,1,0:T(8,128)(2,1)}), bf16[6,2048,128]{2,1,0:T(8,128)(2,1)}) %all-gather.2.cloned.1.call-update) | async-done | bytes 3145744 | tf_op jit(solution)/shard_map/all_gather | solution.py:105
  62.8 2.9 %convolution_bitcast_fusion = f32[128,6,256]{0,2,1:T(8,128)S(1)} fusion(bf16[6,2048,128]{2,1,0:T(8,128)(2,1)} %all-gather.2.cloned.1.call-done, bf16[2048,128]{0,1:T(8,128)(2,1)S(1)} %get-tuple-element.20, bf16[2048,128]{0,1:T(8,128)(2,1)S(1)} %get-tuple-element.19), kind=kOutput, calls=%fused_computation.13 | convolution fusion | flops 807403520 | bytes 4980736 | tf_op jit(solution)/shard_map/stc,tf->csf/dot_general | solution.py:103
  66.2 3.1 %collective-permute-start = (bf16[128,1536]{1,0:T(8,128)(2,1)S(1)}, bf16[128,1536]{1,0:T(8,128)(2,1)}, u32[]{:S(2)}, u32[]{:S(2)}) collective-permute-start(bf16[128,1536]{1,0:T(8,128)(2,1)S(1)} %copy.20), channel_id=1, source_target_pairs={{0,8},{2,10},{4,12},{6,14},{8,16},{10,18},{12,20},{14,22},{16,24},... | collective-permute-start | bytes 1179656 | tf_op jit(solution)/shard_map/ppermute | solution.py:15
  69.9 6.0 %collective-permute-start.3 = (bf16[128,1536]{1,0:T(8,128)(2,1)S(1)}, bf16[128,1536]{1,0:T(8,128)(2,1)S(1)}, u32[]{:S(2)}, u32[]{:S(2)}) collective-permute-start(bf16[128,1536]{1,0:T(8,128)(2,1)S(1)} %copy.20), channel_id=1, source_target_pairs={{0,254},{2,0},{4,2},{6,4},{8,6},{10,8},{12,10},{14,12},{16,14},{18... | collective-permute-start | bytes 1179656 | tf_op jit(solution)/shard_map/ppermute | solution.py:15
  75.8 1.4 collective-permute-start.4
  77.9 13.2 %subtract_convert_fusion = (bf16[16,128,6,1,128]{4,3,2,1,0:T(2,128)(2,1)S(1)}, bf16[16,128,6,1,128]{4,3,2,1,0:T(2,128)(2,1)S(1)}) fusion(f32[16,128]{1,0:T(8,128)S(1)} %get-tuple-element.18, f32[128,6,128]{2,1,0:T(8,128)S(1)} %copy.19, f32[16,128]{1,0:T(8,128)S(1)} %get-tuple-element.17, f32[128,6,128]{2,1,0:T(8,128)S(1)} %copy.18), kind=kLoop, calls=%fused_computation.6 | loop fusion | flops 12582912 | bytes 7094272 | tf_op jit(solution)/shard_map/convert.1
  91.1 15.4 %pad_maximum_fusion = bf16[16,128,6,2,128]{4,3,2,1,0:T(2,128)(2,1)} fusion(bf16[16,128,6,1,128]{4,3,2,1,0:T(2,128)(2,1)S(1)} %get-tuple-element.10, bf16[16,128,6,1,128]{4,3,2,1,0:T(2,128)(2,1)S(1)} %get-tuple-element.9), kind=kLoop, calls=%fused_computation.1 | loop fusion | flops 12582912 | bytes 12582912 | tf_op jit(solution)/shard_map/stack | solution.py:76
  106.5 14.4 %reshape.152 = bf16[16,128,1536,1]{2,1,0,3:T(8,128)(2,1)} reshape(bf16[16,128,6,2,128]{4,3,2,1,0:T(2,128)(2,1)} %pad_maximum_fusion) | data formatting | bytes 12582912 | tf_op jit(solution)/shard_map/convert_element_type | solution.py:77
  121.2 1.8 %bitcast_dynamic-update-slice_fusion.5 = bf16[6,128,1536]{2,1,0:T(8,128)(2,1)} fusion(bf16[128,1536]{1,0:T(8,128)(2,1)} %collective-permute-done), kind=kLoop, calls=%fused_computation.38 | loop fusion | bytes 786432
  123.0 0.8 bitcast_dynamic-update-slice_fusion.4
  123.8 0.8 bitcast_dynamic-update-slice_fusion.3
  124.6 0.8 bitcast_dynamic-update-slice_fusion.2
  125.3 0.8 bitcast_dynamic-update-slice_fusion.1
  126.1 6.3 %collective-permute-done.5 = bf16[128,1536]{1,0:T(8,128)(2,1)S(1)} collective-permute-done((bf16[128,1536]{1,0:T(8,128)(2,1)S(1)}, bf16[128,1536]{1,0:T(8,128)(2,1)S(1)}, u32[]{:S(2)}, u32[]{:S(2)}) %collective-permute-start.5) | collective-permute-done | bytes 393248 | tf_op jit(solution)/shard_map/ppermute | solution.py:15
  132.4 0.8 bitcast_dynamic-update-slice_fusion
  133.2 2.4 %gather_fusion = bf16[6,128,1536]{2,1,0:T(8,128)(2,1)S(1)} fusion(bf16[6,128,1536]{2,1,0:T(8,128)(2,1)} %bitcast_dynamic-update-slice_fusion, s32[1024]{0:T(1024)S(1)} %pad_clamp_fusion), kind=kCustom, calls=%fused_computation | custom fusion | bytes 4718616 | tf_op jit(solution)/shard_map/jit(_take)/gather | solution.py:122
  135.5 0.8 multiply_reduce_fusion
  136.3 7.4 %multiply_bitcast_fusion = f32[6,16,128,128]{3,2,0,1:T(8,128)S(1)} fusion(f32[6,128]{1,0:T(8,128)S(1)} %add_rsqrt_fusion, f32[128]{0:T(128)S(1)} %add_rsqrt_fusion.1, bf16[16,128,1536,1]{2,1,0,3:T(8,128)(2,1)} %reshape.152, bf16[6,128,1536]{2,1,0:T(8,128)(2,1)S(1)} %gather_fusion, pred[6]{0:T(512)(128)(4,1)S(1)} %get-tuple-element.7), kind=kOutput, calls=%fused_computation.4 | convolution fusion | flops 4837736448 | bytes 14945798 | tf_op jit(solution)/shard_map/dot_general | solution.py:83
  143.7 3.1 %copy.26 = f32[6,16,128,128]{3,2,1,0:T(8,128)} copy(f32[6,16,128,128]{3,2,0,1:T(8,128)S(1)} %multiply_bitcast_fusion) | data formatting | bytes 12582912 | tf_op jit(solution)/shard_map/mul | solution.py:88
  (27 shorter events, 3.6 us)
Async XLA Ops:
  6.5 4.1 %copy-start = (f32[16,128]{1,0:T(8,128)S(1)}, f32[16,128]{1,0:T(8,128)}, u32[]{:S(2)}) copy-start(f32[16,128]{1,0:T(8,128)} %param.7) | copy-start | bytes 24580
  6.5 56.2 %all-gather.2.cloned.1.call-start = ((), (), s32[]{:S(2)}) async-start(), calls=%async_computation | async-start | bytes 4718592 | tf_op jit(solution)/shard_map/all_gather | solution.py:105
  66.2 54.7 %collective-permute-start = (bf16[128,1536]{1,0:T(8,128)(2,1)S(1)}, bf16[128,1536]{1,0:T(8,128)(2,1)}, u32[]{:S(2)}, u32[]{:S(2)}) collective-permute-start(bf16[128,1536]{1,0:T(8,128)(2,1)S(1)} %copy.20), channel_id=1, source_target_pairs={{0,8},{2,10},{4,12},{6,14},{8,16},{10,18},{12,20},{14,22},{16,24},... | collective-permute-start | bytes 1179656 | tf_op jit(solution)/shard_map/ppermute | solution.py:15
  69.3 53.7 %collective-permute-start.1 = (bf16[128,1536]{1,0:T(8,128)(2,1)S(1)}, bf16[128,1536]{1,0:T(8,128)(2,1)S(1)}, u32[]{:S(2)}, u32[]{:S(2)}) collective-permute-start(bf16[128,1536]{1,0:T(8,128)(2,1)S(1)} %copy.20), channel_id=1, source_target_pairs={{0,4},{2,6},{4,8},{6,10},{8,12},{10,14},{12,16},{14,18},{16,20},{1... | collective-permute-start | bytes 1179656 | tf_op jit(solution)/shard_map/ppermute | solution.py:15
  69.9 53.9 %collective-permute-start.2 = (bf16[128,1536]{1,0:T(8,128)(2,1)S(1)}, bf16[128,1536]{1,0:T(8,128)(2,1)S(1)}, u32[]{:S(2)}, u32[]{:S(2)}) collective-permute-start(bf16[128,1536]{1,0:T(8,128)(2,1)S(1)} %copy.20), channel_id=1, source_target_pairs={{0,2},{2,4},{4,6},{6,8},{8,10},{10,12},{12,14},{14,16},{16,18},{18... | collective-permute-start | bytes 1179656 | tf_op jit(solution)/shard_map/ppermute | solution.py:15
  69.9 54.7 %collective-permute-start.3 = (bf16[128,1536]{1,0:T(8,128)(2,1)S(1)}, bf16[128,1536]{1,0:T(8,128)(2,1)S(1)}, u32[]{:S(2)}, u32[]{:S(2)}) collective-permute-start(bf16[128,1536]{1,0:T(8,128)(2,1)S(1)} %copy.20), channel_id=1, source_target_pairs={{0,254},{2,0},{4,2},{6,4},{8,6},{10,8},{12,10},{14,12},{16,14},{18... | collective-permute-start | bytes 1179656 | tf_op jit(solution)/shard_map/ppermute | solution.py:15
  75.8 49.5 %collective-permute-start.4 = (bf16[128,1536]{1,0:T(8,128)(2,1)S(1)}, bf16[128,1536]{1,0:T(8,128)(2,1)S(1)}, u32[]{:S(2)}, u32[]{:S(2)}) collective-permute-start(bf16[128,1536]{1,0:T(8,128)(2,1)S(1)} %copy.20), channel_id=1, source_target_pairs={{0,252},{2,254},{4,0},{6,2},{8,4},{10,6},{12,8},{14,10},{16,12},{1... | collective-permute-start | bytes 1179656 | tf_op jit(solution)/shard_map/ppermute | solution.py:15
  120.9 11.5 %collective-permute-start.5 = (bf16[128,1536]{1,0:T(8,128)(2,1)S(1)}, bf16[128,1536]{1,0:T(8,128)(2,1)S(1)}, u32[]{:S(2)}, u32[]{:S(2)}) collective-permute-start(bf16[128,1536]{1,0:T(8,128)(2,1)S(1)} %copy.20), channel_id=1, source_target_pairs={{0,248},{2,250},{4,252},{6,254},{8,0},{10,2},{12,4},{14,6},{16,8},... | collective-permute-start | bytes 1179656 | tf_op jit(solution)/shard_map/ppermute | solution.py:15
Sparse Core Ops, SparseCore 0:
  9.2 53.5 all-gather.1
where the time goes:
time: 154 us
  waiting for transfers between devices  53.5 us (35%)
  other arithmetic  36.1 us (23%)
  local copies, waits for them, and re-layouts  26.2 us (17%)
  between operations  13.5 us (9%)
  matrix products  12.8 us (8%)
  starting transfers between devices  11.4 us (7%)
    all_gather x1, waiting for transfers between devices, local(): lax.all_gather(records, 'tm', axis=0, tiled=True)  46.5 us
    another operation x2, other arithmetic  18.1 us
    another operation x1, other arithmetic, turned_rows(): stacked = jnp.stack([new_real, new_imag], axis=3)  15.4 us
    convert_element_type x1, local copies, waits for them, and re-layouts, turned_rows(): stacked.astype(jnp.bfloat16)  14.4 us
    ppermute x6, starting transfers between devices, shifted(): return lax.ppermute(value, axis, pairs)  11.4 us
    dot_general x1, matrix products, tile_sums(): lax.dot_general(turned, flat_rows, (((1,), (1,)), ((), ())), preferred_el...  7.36 us
    ppermute x6, waiting for transfers between devices, shifted(): return lax.ppermute(value, axis, pairs)  6.29 us
    unnamed x7, local copies, waits for them, and re-layouts  4.86 us
  transfers between devices with their start and end apart: 7, of which 2 were waited for; matrix products, arithmetic and copies ran while one was open for 37% of the time, Pallas kernels for 0%

commit v1 on v0

--- a/solution.py
+++ b/solution.py
@@ -102,7 +102,9 @@
     live_values = live_mask.astype(jnp.float32)
     raw_spec = jnp.einsum(
         "stc,tf->csf",
-        lax.all_gather(records, "tm", axis=0, tiled=True),
+        jnp.concatenate(
+            lax.all_to_all(jnp.stack([records] * lax.axis_size("tm")), "tm", 0, 0), axis=0
+        ),
         transform,
         preferred_element_type=jnp.float32,
     )

time: 154 us -> 130 us (0.84)
  waiting for transfers between devices: 53.5 us -> 35.2 us
  between operations: 13.5 us -> 0.21 us
  starting transfers between devices: 11.4 us -> 17.5 us
  other arithmetic: 36.1 us -> 39.5 us
  matrix products: 12.8 us -> 10.8 us
    all_gather x1 -> x0, waiting for transfers between devices: 46.5 us -> none  [local(): lax.all_gather(records, 'tm', axis=0, tiled=True)]
    all_to_all x0 -> x1, waiting for transfers between devices: none -> 30.6 us  [local(): lax.all_to_all(jnp.stack([records] * lax.axis_size('tm')), 'tm', 0, 0)]
    another operation x2 -> x3, other arithmetic: 18.1 us -> 22.8 us
    all_to_all x0 -> x1, starting transfers between devices: none -> 4.08 us  [local(): lax.all_to_all(jnp.stack([records] * lax.axis_size('tm')), 'tm', 0, 0)]
    ppermute x6, starting transfers between devices: 11.4 us -> 13.4 us  [shifted(): return lax.ppermute(value, axis, pairs)]
    ppermute x6, waiting for transfers between devices: 6.29 us -> 4.6 us  [shifted(): return lax.ppermute(value, axis, pairs)]
    unnamed x7 -> x13, local copies, waits for them, and re-layouts: 4.86 us -> 4.87 us
  transfers between devices with their start and end apart: 7 -> 7, of which waited for: 2 -> 2; matrix products, arithmetic and copies ran while one was open for 37% -> 43% of each run, Pallas kernels for 0% -> 0%
where the time goes in v1:
time: 130 us; the launch traced here: 129 us
  other arithmetic  39.5 us (30%)
  waiting for transfers between devices  35.2 us (27%)
  local copies, waits for them, and re-layouts  26.3 us (20%)
  starting transfers between devices  17.5 us (13%)
  matrix products  10.8 us (8%)
    all_to_all x1, waiting for transfers between devices, local(): lax.all_to_all(jnp.stack([records] * lax.axis_size('tm')), 'tm', 0, 0)  30.6 us
    another operation x2, other arithmetic  18.9 us
    another operation x1, other arithmetic, turned_rows(): stacked = jnp.stack([new_real, new_imag], axis=3)  15.4 us
    convert_element_type x1, local copies, waits for them, and re-layouts, turned_rows(): stacked.astype(jnp.bfloat16)  14.4 us
    ppermute x6, starting transfers between devices, shifted(): return lax.ppermute(value, axis, pairs)  13.4 us
    dot_general x1, matrix products, tile_sums(): lax.dot_general(turned, flat_rows, (((1,), (1,)), ((), ())), preferred_el...  7.36 us
    unnamed x13, local copies, waits for them, and re-layouts  4.87 us
    ppermute x6, waiting for transfers between devices, shifted(): return lax.ppermute(value, axis, pairs)  4.6 us
  transfers between devices with their start and end apart: 7, of which 2 were waited for; matrix products, arithmetic and copies ran while one was open for 43% of the time, Pallas kernels for 0%

profile of v1, /device:TPU:2, one launch (start us, length us, event | category | flops | bytes accessed | tf_op | source)
XLA Modules:
  0.0 129.5 jit_solution(1346958241435718699)
XLA Ops:
  0.0 3.8 %pad_maximum_fusion.1 = bf16[2,3,2048,128]{3,2,1,0:T(8,128)(2,1)} fusion(bf16[1,3,2048,128]{3,2,1,0:T(8,128)(2,1)} %bitcast.61), kind=kLoop, calls=%fused_computation.8 | loop fusion | flops 1572864 | bytes 4718592 | tf_op jit(solution)/shard_map/stack | solution.py:106
  3.9 4.1 %all-to-all-start = ((bf16[2,3,2048,128]{3,2,1,0:T(8,128)(2,1)}), bf16[2,3,2048,128]{3,2,1,0:T(8,128)(2,1)S(1)}, u32[]{:S(2)}, u32[]{:S(2)}) async-start(bf16[2,3,2048,128]{3,2,1,0:T(8,128)(2,1)} %pad_maximum_fusion.1), calls=%async_computation | async-start | bytes 6291456 | tf_op jit(solution)/shard_map/all_to_all | solution.py:106
  9.5 5.7 %cosine_convert_fusion = (bf16[2048,128]{0,1:T(8,128)(2,1)}, bf16[2048,128]{0,1:T(8,128)(2,1)}) fusion(s32[128]{0:T(128)S(1)} %multiply_add_fusion), kind=kLoop, calls=%fused_computation.26 | loop fusion | flops 4456448 | bytes 1049088 | tf_op jit(solution)/shard_map/convert.3
  15.2 30.6 %all-to-all-done = bf16[2,3,2048,128]{3,2,1,0:T(8,128)(2,1)S(1)} async-done(((bf16[2,3,2048,128]{3,2,1,0:T(8,128)(2,1)}), bf16[2,3,2048,128]{3,2,1,0:T(8,128)(2,1)S(1)}, u32[]{:S(2)}, u32[]{:S(2)}) %all-to-all-start) | async-done | bytes 3145760 | tf_op jit(solution)/shard_map/all_to_all | solution.py:106
  45.8 2.2 %convolution_bitcast_fusion = f32[128,6,256]{0,2,1:T(8,128)S(1)} fusion(bf16[6,2048,128]{2,1,0:T(8,128)(2,1)S(1)} %bitcast.60, bf16[2048,128]{0,1:T(8,128)(2,1)} %get-tuple-element.20, bf16[2048,128]{0,1:T(8,128)(2,1)} %get-tuple-element.19), kind=kOutput, calls=%fused_computation.14 | convolution fusion | flops 807403520 | bytes 4980736 | tf_op jit(solution)/shard_map/stc,tf->csf/dot_general | solution.py:103
  48.5 3.3 %collective-permute-start = (bf16[128,1536]{1,0:T(8,128)(2,1)S(1)}, bf16[128,1536]{1,0:T(8,128)(2,1)}, u32[]{:S(2)}, u32[]{:S(2)}) collective-permute-start(bf16[128,1536]{1,0:T(8,128)(2,1)S(1)} %copy.11), channel_id=1, source_target_pairs={{0,8},{2,10},{4,12},{6,14},{8,16},{10,18},{12,20},{14,22},{16,24},... | collective-permute-start | bytes 1179656 | tf_op jit(solution)/shard_map/ppermute | solution.py:15
  51.8 0.7 collective-permute-start.1
  52.5 6.0 %collective-permute-start.3 = (bf16[128,1536]{1,0:T(8,128)(2,1)S(1)}, bf16[128,1536]{1,0:T(8,128)(2,1)S(1)}, u32[]{:S(2)}, u32[]{:S(2)}) collective-permute-start(bf16[128,1536]{1,0:T(8,128)(2,1)S(1)} %copy.11), channel_id=1, source_target_pairs={{0,254},{2,0},{4,2},{6,4},{8,6},{10,8},{12,10},{14,12},{16,14},{18... | collective-permute-start | bytes 1179656 | tf_op jit(solution)/shard_map/ppermute | solution.py:15
  58.5 1.3 %collective-permute-start.4 = (bf16[128,1536]{1,0:T(8,128)(2,1)S(1)}, bf16[128,1536]{1,0:T(8,128)(2,1)S(1)}, u32[]{:S(2)}, u32[]{:S(2)}) collective-permute-start(bf16[128,1536]{1,0:T(8,128)(2,1)S(1)} %copy.11), channel_id=1, source_target_pairs={{0,252},{2,254},{4,0},{6,2},{8,4},{10,6},{12,8},{14,10},{16,12},{1... | collective-permute-start | bytes 1179656 | tf_op jit(solution)/shard_map/ppermute | solution.py:15
  60.4 13.2 %subtract_convert_fusion = (bf16[16,128,6,1,128]{4,3,2,1,0:T(2,128)(2,1)S(1)}, bf16[16,128,6,1,128]{4,3,2,1,0:T(2,128)(2,1)S(1)}) fusion(f32[16,128]{1,0:T(8,128)S(1)} %get-tuple-element.18, f32[128,6,128]{2,1,0:T(8,128)S(1)} %copy.10, f32[16,128]{1,0:T(8,128)S(1)} %get-tuple-element.17, f32[128,6,128]{2,1,0:T(8,128)S(1)} %copy.9), kind=kLoop, calls=%fused_computation.6 | loop fusion | flops 12582912 | bytes 7094272 | tf_op jit(solution)/shard_map/convert.1
  73.7 15.4 %pad_maximum_fusion = bf16[16,128,6,2,128]{4,3,2,1,0:T(2,128)(2,1)} fusion(bf16[16,128,6,1,128]{4,3,2,1,0:T(2,128)(2,1)S(1)} %get-tuple-element.10, bf16[16,128,6,1,128]{4,3,2,1,0:T(2,128)(2,1)S(1)} %get-tuple-element.9), kind=kLoop, calls=%fused_computation.1 | loop fusion | flops 12582912 | bytes 12582912 | tf_op jit(solution)/shard_map/stack | solution.py:76
  89.0 14.4 %reshape.156 = bf16[16,128,1536,1]{2,1,0,3:T(8,128)(2,1)} reshape(bf16[16,128,6,2,128]{4,3,2,1,0:T(2,128)(2,1)} %pad_maximum_fusion) | data formatting | bytes 12582912 | tf_op jit(solution)/shard_map/convert_element_type | solution.py:77
  103.5 2.1 %collective-permute-start.5 = (bf16[128,1536]{1,0:T(8,128)(2,1)S(1)}, bf16[128,1536]{1,0:T(8,128)(2,1)S(1)}, u32[]{:S(2)}, u32[]{:S(2)}) collective-permute-start(bf16[128,1536]{1,0:T(8,128)(2,1)S(1)} %copy.11), channel_id=1, source_target_pairs={{0,248},{2,250},{4,252},{6,254},{8,0},{10,2},{12,4},{14,6},{16,8},... | collective-permute-start | bytes 1179656 | tf_op jit(solution)/shard_map/ppermute | solution.py:15
  105.6 1.8 %bitcast_dynamic-update-slice_fusion.5 = bf16[6,128,1536]{2,1,0:T(8,128)(2,1)} fusion(bf16[128,1536]{1,0:T(8,128)(2,1)} %collective-permute-done), kind=kLoop, calls=%fused_computation.39 | loop fusion | bytes 786432
  107.4 0.8 bitcast_dynamic-update-slice_fusion.4
  108.1 0.8 bitcast_dynamic-update-slice_fusion.3
  108.9 0.8 bitcast_dynamic-update-slice_fusion.2
  109.7 0.8 bitcast_dynamic-update-slice_fusion.1
  110.5 4.6 %collective-permute-done.5 = bf16[128,1536]{1,0:T(8,128)(2,1)S(1)} collective-permute-done((bf16[128,1536]{1,0:T(8,128)(2,1)S(1)}, bf16[128,1536]{1,0:T(8,128)(2,1)S(1)}, u32[]{:S(2)}, u32[]{:S(2)}) %collective-permute-start.5) | collective-permute-done | bytes 393248 | tf_op jit(solution)/shard_map/ppermute | solution.py:15
  115.0 0.8 bitcast_dynamic-update-slice_fusion
  115.8 2.4 %gather_fusion = bf16[6,128,1536]{2,1,0:T(8,128)(2,1)S(1)} fusion(bf16[6,128,1536]{2,1,0:T(8,128)(2,1)} %bitcast_dynamic-update-slice_fusion, s32[1024]{0:T(1024)S(1)} %pad_clamp_fusion), kind=kCustom, calls=%fused_computation | custom fusion | bytes 4718616 | tf_op jit(solution)/shard_map/jit(_take)/gather | solution.py:124
  118.2 0.8 multiply_reduce_fusion
  118.9 7.4 %multiply_bitcast_fusion = f32[6,16,128,128]{3,2,0,1:T(8,128)S(1)} fusion(f32[6,128]{1,0:T(8,128)S(1)} %add_rsqrt_fusion, f32[128]{0:T(128)S(1)} %add_rsqrt_fusion.1, bf16[16,128,1536,1]{2,1,0,3:T(8,128)(2,1)} %reshape.156, bf16[6,128,1536]{2,1,0:T(8,128)(2,1)S(1)} %gather_fusion, pred[6]{0:T(512)(128)(4,1)S(1)} %get-tuple-element.7), kind=kOutput, calls=%fused_computation.4 | convolution fusion | flops 4837736448 | bytes 14945798 | tf_op jit(solution)/shard_map/dot_general | solution.py:83
  126.3 3.1 %copy.17 = f32[6,16,128,128]{3,2,1,0:T(8,128)} copy(f32[6,16,128,128]{3,2,0,1:T(8,128)S(1)} %multiply_bitcast_fusion) | data formatting | bytes 12582912 | tf_op jit(solution)/shard_map/mul | solution.py:88
  (33 shorter events, 2.6 us)
Async XLA Ops:
  0.0 8.8 %copy-start = (f32[16,128]{1,0:T(8,128)S(1)}, f32[16,128]{1,0:T(8,128)}, u32[]{:S(2)}) copy-start(f32[16,128]{1,0:T(8,128)} %param.7) | copy-start | bytes 24580
  3.8 4.1 %copy-start.2 = (s32[128]{0:T(128)S(1)}, s32[128]{0:T(128)}, u32[]{:S(2)}) copy-start(s32[128]{0:T(128)} %param.8) | copy-start | bytes 1540
  3.9 4.1 %copy-start.1 = (s32[6,1]{0,1:T(1,128)S(1)}, s32[6,1]{0,1:T(1,128)}, u32[]{:S(2)}) copy-start(s32[6,1]{0,1:T(1,128)} %param.9) | copy-start | bytes 76
  3.9 4.2 %copy-start.3 = (f32[64]{0:T(128)S(1)}, f32[64]{0:T(128)}, u32[]{:S(2)}) copy-start(f32[64]{0:T(128)} %param.6) | copy-start | bytes 772
  3.9 41.9 %all-to-all-start = ((bf16[2,3,2048,128]{3,2,1,0:T(8,128)(2,1)}), bf16[2,3,2048,128]{3,2,1,0:T(8,128)(2,1)S(1)}, u32[]{:S(2)}, u32[]{:S(2)}) async-start(bf16[2,3,2048,128]{3,2,1,0:T(8,128)(2,1)} %pad_maximum_fusion.1), calls=%async_computation | async-start | bytes 6291456 | tf_op jit(solution)/shard_map/all_to_all | solution.py:106
  48.5 54.9 %collective-permute-start = (bf16[128,1536]{1,0:T(8,128)(2,1)S(1)}, bf16[128,1536]{1,0:T(8,128)(2,1)}, u32[]{:S(2)}, u32[]{:S(2)}) collective-permute-start(bf16[128,1536]{1,0:T(8,128)(2,1)S(1)} %copy.11), channel_id=1, source_target_pairs={{0,8},{2,10},{4,12},{6,14},{8,16},{10,18},{12,20},{14,22},{16,24},... | collective-permute-start | bytes 1179656 | tf_op jit(solution)/shard_map/ppermute | solution.py:15
  51.8 55.5 %collective-permute-start.1 = (bf16[128,1536]{1,0:T(8,128)(2,1)S(1)}, bf16[128,1536]{1,0:T(8,128)(2,1)S(1)}, u32[]{:S(2)}, u32[]{:S(2)}) collective-permute-start(bf16[128,1536]{1,0:T(8,128)(2,1)S(1)} %copy.11), channel_id=1, source_target_pairs={{0,4},{2,6},{4,8},{6,10},{8,12},{10,14},{12,16},{14,18},{16,20},{1... | collective-permute-start | bytes 1179656 | tf_op jit(solution)/shard_map/ppermute | solution.py:15
  52.5 55.6 %collective-permute-start.2 = (bf16[128,1536]{1,0:T(8,128)(2,1)S(1)}, bf16[128,1536]{1,0:T(8,128)(2,1)S(1)}, u32[]{:S(2)}, u32[]{:S(2)}) collective-permute-start(bf16[128,1536]{1,0:T(8,128)(2,1)S(1)} %copy.11), channel_id=1, source_target_pairs={{0,2},{2,4},{4,6},{6,8},{8,10},{10,12},{12,14},{14,16},{16,18},{18... | collective-permute-start | bytes 1179656 | tf_op jit(solution)/shard_map/ppermute | solution.py:15
  52.5 56.4 %collective-permute-start.3 = (bf16[128,1536]{1,0:T(8,128)(2,1)S(1)}, bf16[128,1536]{1,0:T(8,128)(2,1)S(1)}, u32[]{:S(2)}, u32[]{:S(2)}) collective-permute-start(bf16[128,1536]{1,0:T(8,128)(2,1)S(1)} %copy.11), channel_id=1, source_target_pairs={{0,254},{2,0},{4,2},{6,4},{8,6},{10,8},{12,10},{14,12},{16,14},{18... | collective-permute-start | bytes 1179656 | tf_op jit(solution)/shard_map/ppermute | solution.py:15
  58.5 51.2 %collective-permute-start.4 = (bf16[128,1536]{1,0:T(8,128)(2,1)S(1)}, bf16[128,1536]{1,0:T(8,128)(2,1)S(1)}, u32[]{:S(2)}, u32[]{:S(2)}) collective-permute-start(bf16[128,1536]{1,0:T(8,128)(2,1)S(1)} %copy.11), channel_id=1, source_target_pairs={{0,252},{2,254},{4,0},{6,2},{8,4},{10,6},{12,8},{14,10},{16,12},{1... | collective-permute-start | bytes 1179656 | tf_op jit(solution)/shard_map/ppermute | solution.py:15
  103.5 11.6 %collective-permute-start.5 = (bf16[128,1536]{1,0:T(8,128)(2,1)S(1)}, bf16[128,1536]{1,0:T(8,128)(2,1)S(1)}, u32[]{:S(2)}, u32[]{:S(2)}) collective-permute-start(bf16[128,1536]{1,0:T(8,128)(2,1)S(1)} %copy.11), channel_id=1, source_target_pairs={{0,248},{2,250},{4,252},{6,254},{8,0},{10,2},{12,4},{14,6},{16,8},... | collective-permute-start | bytes 1179656 | tf_op jit(solution)/shard_map/ppermute | solution.py:15
